TPU v7x, 256 devices: a whole 4x4x8 slice. The times are simulated.
256 devices in a mesh: row: 16 (over y_hi, x, core), col: 16 (over y_lo, z).
Axes of the slice: x: 4, y: 4 (y_hi: 2, y_lo: 2; y = y_hi * 2 + y_lo), z: 8, core: 2. Of those that a mesh axis runs over, the one named last changes fastest.
Arguments:
- tokens: bfloat16 [8192, 6144], P('row', 'col'), may hold values from -6 to 6
- gate_weight: bfloat16 [6144, 12288], P('row', 'col'), may hold values from -0.078125 to 0.078125
- up_weight: bfloat16 [6144, 12288], P('row', 'col'), may hold values from -0.078125 to 0.078125
Outputs:
- hidden: float32 [8192, 12288], P('row', 'col')
All inputs are finite; a program needn't handle non-finite values.
Results may differ from a plain program's by a relative error of at most 0.0003.
Values may be sent and summed in bfloat16 or wider, within the bound.
No kernel may reach another device: no remote copies, remote signals or barrier semaphores. Data moves between devices by JAX's collectives and lax.ppermute only.
A program may use at most 128 MiB of HBM per device.

v0:
```python
import jax
import jax.numpy as jnp
from jax import lax
from jax.sharding import PartitionSpec as P


def accumulate(gathered, weight_rows):
    return jnp.dot(gathered, weight_rows, preferred_element_type=jnp.float32)


def per_device(tokens, gate_weight, up_weight):
    gathered = lax.all_gather(tokens, "col", axis=1, tiled=True)

    def add_single(weight_rows):
        return accumulate(gathered, weight_rows)

    gate_sum = add_single(lax.all_gather(gate_weight, "row", axis=0, tiled=True))
    up_sum = add_single(lax.all_gather(up_weight, "row", axis=0, tiled=True))
    return jax.nn.silu(gate_sum) * up_sum


def solution(mesh):
    in_specs = (P("row", "col"), P("row", "col"), P("row", "col"))
    out_specs = P("row", "col")
    return jax.shard_map(
        per_device, mesh=mesh, in_specs=in_specs, out_specs=out_specs, check_vma=False
    )
```

profile of v0, /device:TPU:1, one launch (start us, length us, event | category | flops | bytes accessed | tf_op | source)
XLA Modules:
  0.0 278.8 jit_solution(5414926896950332376)
XLA Ops:
  6.5 0.0 all-gather.4.cloned.1.call-start
  6.5 0.7 all-gather.4.cloned.1.call-update
  7.3 0.0 all-gather.6.cloned.1.call-start
  7.3 0.7 all-gather.6.cloned.1.call-update
  8.0 0.0 all-gather.8.cloned.1.call-start
  8.1 0.7 all-gather.8.cloned.1.call-update
  8.7 82.3 %all-gather.4.cloned.1.call-done = bf16[512,6144]{1,0:T(8,128)(2,1)} async-done(((bf16[512,384]{1,0:T(8,128)(2,1)}), bf16[512,6144]{1,0:T(8,128)(2,1)}) %all-gather.4.cloned.1.call-update) | async-done | bytes 6291472 | tf_op jit(solution)/shard_map/all_gather | solution.py:12
  91.1 87.6 %all-gather.6.cloned.1.call-done = bf16[6144,768]{1,0:T(8,128)(2,1)} async-done(((bf16[384,768]{1,0:T(8,128)(2,1)}), bf16[6144,768]{1,0:T(8,128)(2,1)}) %all-gather.6.cloned.1.call-update) | async-done | bytes 9437200 | tf_op jit(solution)/shard_map/all_gather | solution.py:17
  178.6 9.3 %fusion = f32[512,768]{1,0:T(8,128)S(1)} fusion(bf16[512,6144]{1,0:T(8,128)(2,1)} %all-gather.4.cloned.1.call-done, bf16[6144,768]{1,0:T(8,128)(2,1)} %all-gather.6.cloned.1.call-done), kind=kOutput, calls=%fused_computation.1 | convolution fusion | flops 4831838208 | bytes 17301504 | tf_op jit(solution)/shard_map/dot_general | solution.py:8
  188.0 73.5 %all-gather.8.cloned.1.call-done = bf16[6144,768]{1,0:T(8,128)(2,1)} async-done(((bf16[384,768]{1,0:T(8,128)(2,1)}), bf16[6144,768]{1,0:T(8,128)(2,1)}) %all-gather.8.cloned.1.call-update) | async-done | bytes 9437200 | tf_op jit(solution)/shard_map/all_gather | solution.py:18
  261.5 10.7 %multiply_multiply_fusion = f32[512,768]{1,0:T(8,128)} fusion(f32[512,768]{1,0:T(8,128)S(1)} %fusion, bf16[512,6144]{1,0:T(8,128)(2,1)} %all-gather.4.cloned.1.call-done, bf16[6144,768]{1,0:T(8,128)(2,1)} %all-gather.8.cloned.1.call-done), kind=kOutput, calls=%fused_computation | convolution fusion | flops 4833804288 | bytes 18874368 | tf_op jit(solution)/shard_map/dot_general | solution.py:8
Async XLA Ops:
  6.5 84.5 %all-gather.4.cloned.1.call-start = ((), (), s32[]{:S(2)}) async-start(), calls=%async_computation | async-start | bytes 6684672 | tf_op jit(solution)/shard_map/all_gather | solution.py:12
  7.3 171.4 %all-gather.6.cloned.1.call-start = ((), (), s32[]{:S(2)}) async-start(), calls=%async_computation.1 | async-start | bytes 10027008 | tf_op jit(solution)/shard_map/all_gather | solution.py:17
  8.0 253.5 %all-gather.8.cloned.1.call-start = ((), (), s32[]{:S(2)}) async-start(), calls=%async_computation.2 | async-start | bytes 10027008 | tf_op jit(solution)/shard_map/all_gather | solution.py:18
Sparse Core Ops, SparseCore 0:
  9.2 81.8 all-gather.3
  93.8 84.7 all-gather.5
  181.4 80.0 all-gather.7
where the time goes:
time: 279 us
  waiting for transfers between devices  246 us (88%)
  matrix products  20.1 us (7%)
  between operations  13.1 us (5%)
    all_gather x1, waiting for transfers between devices, per_device(): lax.all_gather(gate_weight, 'row', axis=0, tiled=True)  87.6 us
    all_gather x1, waiting for transfers between devices, per_device(): gathered = lax.all_gather(tokens, 'col', axis=1, tiled=True)  82.3 us
    all_gather x1, waiting for transfers between devices, per_device(): up_sum = add_single(lax.all_gather(up_weight, 'row', axis=0, tiled=True))  73.5 us
    dot_general x2, matrix products, accumulate(): return jnp.dot(gathered, weight_rows, preferred_element_type=jnp.float32)  20.1 us
  transfers between devices with their start and end apart: 3, of which 3 were waited for; matrix products, arithmetic and copies ran while one was open for 3% of the time, Pallas kernels for 0%

commit v1 on v0

--- a/solution.py
+++ b/solution.py
@@ -2,6 +2,12 @@
 import jax.numpy as jnp
 from jax import lax
 from jax.sharding import PartitionSpec as P
+
+
+def lift_chunk(t0):
+    return jnp.concatenate(
+        lax.all_to_all(jnp.stack([t0 for _ in range(lax.axis_size("row"))]), "row", 0, 0), axis=0
+    )
 
 
 def accumulate(gathered, weight_rows):
@@ -14,7 +20,7 @@
     def add_single(weight_rows):
         return accumulate(gathered, weight_rows)
 
-    gate_sum = add_single(lax.all_gather(gate_weight, "row", axis=0, tiled=True))
+    gate_sum = add_single(lift_chunk(gate_weight))
     up_sum = add_single(lax.all_gather(up_weight, "row", axis=0, tiled=True))
     return jax.nn.silu(gate_sum) * up_sum
 

time: 279 us -> 269 us (0.964)
  waiting for transfers between devices: 246 us -> 52.3 us
  blocking collectives: 0 us -> 181 us
    all_to_all x0 -> x1, blocking collectives: none -> 181 us  [lift_chunk(): lax.all_to_all(jnp.stack([t0 for _ in range(lax.axis_size('row'))]), 'row...]
    all_gather x1 -> x0, waiting for transfers between devices: 87.6 us -> none  [per_device(): lax.all_gather(gate_weight, 'row', axis=0, tiled=True)]
    all_gather x1, waiting for transfers between devices: 82.3 us -> 0.01 us  [per_device(): gathered = lax.all_gather(tokens, 'col', axis=1, tiled=True)]
    all_gather x1, waiting for transfers between devices: 73.5 us -> 50.9 us  [per_device(): up_sum = add_single(lax.all_gather(up_weight, 'row', axis=0, tiled=True))]
  transfers between devices with their start and end apart: 3 -> 2, of which waited for: 3 -> 1; matrix products, arithmetic and copies ran while one was open for 3% -> 4% of each run, Pallas kernels for 0% -> 0%
where the time goes in v1:
time: 269 us
  blocking collectives  181 us (67%)
  waiting for transfers between devices  52.3 us (19%)
  matrix products  20.1 us (7%)
  between operations  13.4 us (5%)
    all_to_all x1, blocking collectives, lift_chunk(): lax.all_to_all(jnp.stack([t0 for _ in range(lax.axis_size('row'))]), 'row...  181 us
    all_gather x1, waiting for transfers between devices, per_device(): up_sum = add_single(lax.all_gather(up_weight, 'row', axis=0, tiled=True))  50.9 us
    dot_general x2, matrix products, accumulate(): return jnp.dot(gathered, weight_rows, preferred_element_type=jnp.float32)  20.1 us
  transfers between devices with their start and end apart: 2, of which 1 were waited for; matrix products, arithmetic and copies ran while one was open for 4% of the time, Pallas kernels for 0%

profile of v1, /device:TPU:1, one launch (start us, length us, event | category | flops | bytes accessed | tf_op | source)
XLA Modules:
  0.0 268.8 jit_solution(14696800534953230165)
XLA Ops:
  6.5 0.0 all-gather.3.cloned.1.call-start
  6.5 0.7 all-gather.3.cloned.1.call-update
  7.3 0.0 all-gather.5.cloned.1.call-start
  7.3 0.7 all-gather.5.cloned.1.call-update
  8.0 2.0 stack.2
  10.0 180.9 %all_to_all.5 = bf16[16,384,768]{2,1,0:T(8,128)(2,1)} all-to-all(bf16[16,384,768]{2,1,0:T(8,128)(2,1)S(1)} %stack.2), channel_id=1, replica_groups=mesh['row'=16,'col'=16] {'row'}, dimensions={0} | all-to-all | bytes 18874368 | tf_op jit(solution)/shard_map/all_to_all | solution.py:9
  190.9 0.0 all-gather.3.cloned.1.call-done
  190.9 9.4 %fusion = f32[512,768]{1,0:T(8,128)S(1)} fusion(bf16[512,6144]{1,0:T(8,128)(2,1)} %all-gather.3.cloned.1.call-done, bf16[6144,768]{1,0:T(8,128)(2,1)} %bitcast.5), kind=kOutput, calls=%fused_computation.1 | convolution fusion | flops 4831838208 | bytes 17301504 | tf_op jit(solution)/shard_map/dot_general | solution.py:14
  200.3 50.9 %all-gather.5.cloned.1.call-done = bf16[6144,768]{1,0:T(8,128)(2,1)} async-done(((bf16[384,768]{1,0:T(8,128)(2,1)}), bf16[6144,768]{1,0:T(8,128)(2,1)}) %all-gather.5.cloned.1.call-update) | async-done | bytes 9437200 | tf_op jit(solution)/shard_map/all_gather | solution.py:24
  251.2 10.7 %multiply_multiply_fusion = f32[512,768]{1,0:T(8,128)} fusion(f32[512,768]{1,0:T(8,128)S(1)} %fusion, bf16[512,6144]{1,0:T(8,128)(2,1)} %all-gather.3.cloned.1.call-done, bf16[6144,768]{1,0:T(8,128)(2,1)} %all-gather.5.cloned.1.call-done), kind=kOutput, calls=%fused_computation | convolution fusion | flops 4833804288 | bytes 18874368 | tf_op jit(solution)/shard_map/dot_general | solution.py:14
Async XLA Ops:
  6.5 184.4 %all-gather.3.cloned.1.call-start = ((), (), s32[]{:S(2)}) async-start(), calls=%async_computation.1 | async-start | bytes 6684672 | tf_op jit(solution)/shard_map/all_gather | solution.py:18
  7.3 243.9 %all-gather.5.cloned.1.call-start = ((), (), s32[]{:S(2)}) async-start(), calls=%async_computation.2 | async-start | bytes 10027008 | tf_op jit(solution)/shard_map/all_gather | solution.py:24
Sparse Core Ops, SparseCore 0:
  9.2 155.6 all-gather.2
  167.5 83.6 all-gather.4
